TPU v7x, 256 devices: a whole 4x4x8 slice. The times are simulated.
256 devices in a mesh: sect: 2 (over core), sec: 128 (over z, y, x).
Axes of the slice: x: 4, y: 4, z: 8, core: 2. Of those that a mesh axis runs over, the one named last changes fastest.
Arguments:
- start_vectors: bfloat16 [2, 2, 128, 4, 256, 256], P('sect', None, 'sec'), may hold values from -20 to 20
- left_env: bfloat16 [2, 128, 5, 256, 256], P('sect', 'sec'), may hold values from -0.15625 to 0.15625
- right_env: bfloat16 [2, 128, 5, 256, 256], P('sect', 'sec'), may hold values from -0.375 to 0.375
- pair_mpo: float32 [5, 5, 4, 4], replicated, may hold values from -1.25 to 1.25
Outputs:
- ritz_vector: float32 [2, 2, 128, 4, 256, 256], P('sect', None, 'sec')
- ritz_residual: float32 [2, 2, 128, 4, 256, 256], P('sect', None, 'sec')
- energy: float32 [2, 2], P('sect')
All inputs are finite; a program needn't handle non-finite values.
Results may differ from a plain program's by a relative error of at most 0.0095.
Values may be sent and summed in bfloat16 or wider, within the bound.
A program may use at most 128 MiB of HBM per device.

v0:
```python
import jax
import jax.numpy as jnp
from jax import lax
from jax.sharding import PartitionSpec as P

epsilon = 1e-06
pair_offsets = (0, 1, 1, 2)


def from_behind(value, axis, by):
    length = lax.axis_size(axis)
    return lax.ppermute(value, axis, [(i, (i + by) % length) for i in range(length)])


def padded_2(value, sides, width):
    for axis, dim in sides:
        size, length = (lax.axis_size(axis), value.shape[dim])
        up = [(i, (i + 1) % size) for i in range(size - 1)]
        down = [(j, i) for i, j in up]
        last = lax.slice_in_dim(value, length - width, length, axis=dim)
        leading = lax.slice_in_dim(value, 0, width, axis=dim)
        before = lax.ppermute(last, axis, up)
        after = lax.ppermute(leading, axis, down)
        value = jnp.concatenate([before, value, after], axis=dim)
    return value


def shortened(value):
    return jax.tree.map(lambda a: a.astype(jnp.bfloat16) if a.dtype == jnp.float32 else a, value)


def pair_charges():
    return jnp.array([0, 1, 1, 2], jnp.int32)


def channel_shifts(channels):
    series = jnp.arange(channels, dtype=jnp.int32)
    return jnp.where(series == channels - 2, 1, jnp.where(series == channels - 1, -1, 0)).astype(
        jnp.int32
    )


def masked_mpo(pair_mpo):
    channels = pair_mpo.shape[0]
    shifts = channel_shifts(channels)
    charges = pair_charges()
    change = charges[:, None] - charges[None, :]
    displaced = shifts[:, None] - shifts[None, :]
    allowed = change[None, None, :, :] == displaced[:, :, None, None]
    return jnp.where(allowed, pair_mpo, jnp.float32(0.0))


def sector_masks(sector_ids, sector_total, channels):
    shifts = channel_shifts(channels)
    charges = pair_charges()
    left_target = sector_ids[:, None] + shifts[None, :]
    right_source = sector_ids[:, None] - shifts[None, :]
    right_bond = sector_ids[:, None] + charges[None, :] - 1
    left_keep = (left_target >= 0) & (left_target < sector_total)
    right_keep = (right_source >= 0) & (right_source < sector_total)
    block_keep = (right_bond >= 0) & (right_bond < sector_total)
    return (left_keep, right_keep, block_keep)


def totals(values):
    return jnp.sum(values, axis=(1, 2, 3, 4))


def spread(scalars):
    return scalars[:, None, None, None, None]


def body(start_vectors, left_env, right_env, pair_mpo):
    local_count = left_env.shape[1]
    channels = left_env.shape[2]
    sector_total = local_count * lax.axis_size("sec")
    sector_ids = lax.axis_index("sec") * local_count + jnp.arange(local_count, dtype=jnp.int32)
    left_keep, right_keep, block_keep = sector_masks(sector_ids, sector_total, channels)
    zero_half = jnp.zeros((), jnp.bfloat16)
    left_used = from_behind(left_env, "sect", 1)[0]
    right_used = from_behind(right_env, "sect", -1)[0]
    left_used = jnp.where(left_keep[:, :, None, None], left_used, zero_half)
    right_used = jnp.where(right_keep[:, :, None, None], right_used, zero_half)
    right_padded = padded_2(right_used, (("sec", 0),), 1)
    mpo_kept = masked_mpo(pair_mpo)

    def one_vector(vector_one):
        partials = []
        for spin_pair in range(4):
            offset = pair_offsets[spin_pair]
            chosen = right_padded[offset : offset + local_count]
            partials.append(
                jnp.einsum(
                    "qab,qwcb->qwac",
                    vector_one[:, spin_pair],
                    chosen,
                    preferred_element_type=jnp.float32,
                )
            )
        stacked = jnp.stack(partials, axis=1)
        blended = jnp.einsum(
            "wxts,qsxac->qtwac", mpo_kept, stacked, precision=lax.Precision.HIGHEST
        )
        return blended.astype(jnp.bfloat16)

    def effective_apply(vector_b):
        blended = lax.map(one_vector, vector_b)
        padded = padded_2(shortened(blended[:, :, :, channels - 2 :]), (("sec", 1),), 1)
        upward = padded[:, 2:, :, 0]
        downward = padded[:, :-2, :, 1]
        selected = jnp.concatenate(
            [blended[:, :, :, : channels - 2], upward[:, :, :, None], downward[:, :, :, None]],
            axis=3,
        )
        return jnp.einsum(
            "qwab,vqswbc->vqsac", left_used, selected, preferred_element_type=jnp.float32
        )

    start_f = start_vectors[0].astype(jnp.float32) * block_keep[None, :, :, None, None].astype(
        jnp.float32
    )
    start_sq = lax.psum(totals(start_f * start_f), "sec")
    vector_b = (start_f / spread(jnp.sqrt(start_sq + epsilon))).astype(jnp.bfloat16)
    vector_v = lax.optimization_barrier(vector_b).astype(jnp.float32)
    image_v = effective_apply(vector_b)
    rayleigh = lax.psum(totals(vector_v * image_v), "sec")
    residual_v = image_v - spread(rayleigh) * vector_v
    residual_sq = lax.psum(totals(residual_v * residual_v), "sec")
    second_b = (residual_v / spread(jnp.sqrt(residual_sq + epsilon))).astype(jnp.bfloat16)
    second_v = lax.optimization_barrier(second_b).astype(jnp.float32)
    image_u = effective_apply(second_b)
    coupling, second_diag = lax.psum(
        (totals(vector_v * image_u), totals(second_v * image_u)), "sec"
    )
    half_gap = 0.5 * (second_diag - rayleigh)
    energy = 0.5 * (rayleigh + second_diag) - jnp.sqrt(half_gap * half_gap + coupling * coupling)
    rotation = 0.5 * jnp.arctan2(coupling, half_gap)
    first_coef = jnp.cos(rotation)
    second_coef = -jnp.sin(rotation)
    ritz_vector = spread(first_coef) * vector_v + spread(second_coef) * second_v
    ritz_residual = (
        spread(first_coef) * image_v + spread(second_coef) * image_u - spread(energy) * ritz_vector
    )
    return (ritz_vector[None], ritz_residual[None], energy[None])


def solution(mesh):
    in_specs = (
        P("sect", None, "sec", None, None, None),
        P("sect", "sec", None, None, None),
        P("sect", "sec", None, None, None),
        P(),
    )
    out_specs = (
        P("sect", None, "sec", None, None, None),
        P("sect", None, "sec", None, None, None),
        P("sect", None),
    )
    return jax.shard_map(body, mesh=mesh, in_specs=in_specs, out_specs=out_specs, check_vma=False)
```

profile of v0, /device:TPU:2, one launch (start us, length us, event | category | flops | bytes accessed | tf_op | source)
XLA Modules:
  0.0 1599.8 jit_solution(17880510354098037987)
XLA Ops:
  2.9 346.6 %psum.35 = f32[2]{0:T(128)S(1)} all-reduce(f32[2]{0:T(128)S(1)} %fusion.37), channel_id=1, replica_groups=mesh['sect'=2,'sec'=128] {'sec'}, use_global_device_ids=true, to_apply=%region_1.2 | all-reduce | flops 2 | bytes 16 | tf_op jit(solution)/shard_map/psum | solution.py:122
  349.7 3.1 collective-permute-start.1
  352.8 7.5 collective-permute-start.2
  361.8 4.5 collective-permute-done.1
  366.3 2.2 collective-permute-done.2
  368.4 2.9 broadcast.259.clone.1.clone
  371.4 54.4 %while.20 = (s32[]{:T(128)}, bf16[2,1,4,5,256,256]{4,5,3,2,0,1:T(8,128)(2,1)}, bf16[2,1,4,256,256]{3,4,2,0,1:T(8,128)(2,1)}, bf16[1,5,256,256]{3,2,1,0:T(8,128)(...) while((s32[]{:T(128)}, ...), condition=%wide.region_3.4_spmd, body=%wide.region_2.3_spmd.sunk | while | flops 990904320 | bytes 39323800 | solution.py:107
  376.8 14.6 fusion.70
  391.4 5.5 copy.55
  404.0 14.6 fusion.70
  418.6 5.5 copy.55
  427.7 4.5 collective-permute-start.3
  434.4 2.2 slice.48
  436.6 19.3 %collective-permute-done.3 = bf16[2,1,4,2,256,256]{4,5,3,2,0,1:T(8,128)(2,1)S(1)} collective-permute-done((bf16[2,1,4,2,256,256]{4,5,3,2,0,1:T(8,128)(2,1)S(1)}, bf16[2,1,4,2,256,256]{4,5,3,2,0,1:T(8,128)(2,1)S(1)}, u32[]{:S(2)}, u32[]{:S(2)}) %collective-permute-start.3) | collective-permute-done | bytes 2097184 | tf_op jit(solution)/shard_map/ppermute | solution.py:23
  455.9 4.3 collective-permute-done.4
  460.3 3.2 fusion.32
  463.6 341.7 %psum.36 = f32[2]{0:T(128)S(1)} all-reduce(f32[2]{0:T(128)S(1)} %get-tuple-element.133), channel_id=1, replica_groups=mesh['sect'=2,'sec'=128] {'sec'}, use_global_device_ids=true, to_apply=%region_5.6 | all-reduce | flops 2 | bytes 16 | tf_op jit(solution)/shard_map/psum | solution.py:126
  807.1 344.5 %psum.37 = f32[2]{0:T(128)S(1)} all-reduce(f32[2]{0:T(128)S(1)} %multiply_reduce_fusion), channel_id=1, replica_groups=mesh['sect'=2,'sec'=128] {'sec'}, use_global_device_ids=true, to_apply=%region_7.8 | all-reduce | flops 2 | bytes 16 | tf_op jit(solution)/shard_map/psum | solution.py:128
  1151.7 2.6 divide_convert_fusion
  1154.2 2.9 broadcast.259.clone.1
  1157.2 54.4 %while.21 = (s32[]{:T(128)}, bf16[2,1,4,5,256,256]{4,5,3,2,0,1:T(8,128)(2,1)}, bf16[2,1,4,256,256]{3,4,2,0,1:T(8,128)(2,1)}, bf16[1,5,256,256]{3,2,1,0:T(8,128)(...) while((s32[]{:T(128)}, ...), condition=%wide.region_9.10_spmd, body=%wide.region_8.9_spmd.sunk | while | flops 990904320 | bytes 39323800 | solution.py:107
  1162.6 14.6 fusion.77
  1177.2 5.5 copy.58
  1189.8 14.6 fusion.77
  1204.4 5.5 copy.58
  1215.5 3.7 collective-permute-start.7
  1219.2 2.2 slice.52
  1221.5 20.1 %collective-permute-done.6 = bf16[2,1,4,2,256,256]{4,5,3,2,0,1:T(8,128)(2,1)S(1)} collective-permute-done((bf16[2,1,4,2,256,256]{4,5,3,2,0,1:T(8,128)(2,1)S(1)}, bf16[2,1,4,2,256,256]{4,5,3,2,0,1:T(8,128)(2,1)S(1)}, u32[]{:S(2)}, u32[]{:S(2)}) %collective-permute-start.6) | collective-permute-done | bytes 2097184 | tf_op jit(solution)/shard_map/ppermute | solution.py:23
  1243.8 4.4 fusion.30
  1248.2 341.7 %all-reduce = (f32[2]{0:T(128)S(1)}, f32[2]{0:T(128)S(1)}) all-reduce(f32[2]{0:T(128)S(1)} %get-tuple-element.97, f32[2]{0:T(128)S(1)} %get-tuple-element.96), channel_id=1, replica_groups=mesh['sect'=2,'sec'=128] {'sec'}, use_global_device_ids=true, to_apply=%region_11.12 | all-reduce | flops 4 | bytes 32 | tf_op jit(solution)/shard_map/psum | solution.py:132
  1590.0 4.9 fusion.41
  1595.0 3.0 copy.19
  (84 shorter events, 46.2 us)
Async XLA Ops:
  0.6 1.6 copy-start.5
  0.6 348.8 %copy-start.6 = (s32[4]{0:T(128)S(1)}, s32[4]{0:T(128)}, u32[]{:S(2)}) copy-start(s32[4]{0:T(128)} %constant.52) | copy-start | bytes 52
  0.7 2.2 copy-start.7
  0.7 359.7 %copy-start.3 = (f32[5,5,4,4]{1,3,2,0:T(4,128)S(1)}, f32[5,5,4,4]{1,3,2,0:T(4,128)}, u32[]{:S(2)}) copy-start(f32[5,5,4,4]{1,3,2,0:T(4,128)} %param.13) | copy-start | bytes 4804
  2.8 346.8 %collective-permute-start = (bf16[1,1,5,256,256]{4,3,2,1,0:T(8,128)(2,1)S(1)}, bf16[1,1,5,256,256]{4,3,2,1,0:T(8,128)(2,1)S(1)}, u32[]{:S(2)}, u32[]{:S(2)}) collective-permute-start(bf16[1,1,5,256,256]{4,3,2,1,0:T(8,128)(2,1)S(1)} %copy-done.7), channel_id=1, source_target_pairs={{0,128},{128,0},{1,129},{129,1},{2,130},{130,2},{3,131},{131,3},{4... | collective-permute-start | bytes 1966088 | tf_op jit(solution)/shard_map/ppermute | solution.py:12
  349.7 16.5 %collective-permute-start.1 = (bf16[1,5,256,256]{3,2,1,0:T(8,128)(2,1)S(1)}, bf16[1,5,256,256]{3,2,1,0:T(8,128)(2,1)}, u32[]{:S(2)}, u32[]{:S(2)}) collective-permute-start(bf16[1,5,256,256]{3,2,1,0:T(8,128)(2,1)S(1)} %bitcast_select_fusion.1), channel_id=1, source_target_pairs={{0,1},{1,2},{2,3},{3,4},{4,5},{5,6},{6,7},{7,8},{8,9},{9,10},{10,1... | collective-permute-start | bytes 1966088 | tf_op jit(solution)/shard_map/ppermute | solution.py:22
  352.8 15.6 collective-permute-start.2
  425.8 8.3 copy-start.8
  427.7 28.2 %collective-permute-start.3 = (bf16[2,1,4,2,256,256]{4,5,3,2,0,1:T(8,128)(2,1)S(1)}, bf16[2,1,4,2,256,256]{4,5,3,2,0,1:T(8,128)(2,1)S(1)}, u32[]{:S(2)}, u32[]{:S(2)}) collective-permute-start(bf16[2,1,4,2,256,256]{4,5,3,2,0,1:T(8,128)(2,1)S(1)} %slice.49), channel_id=1, source_target_pairs={{1,0},{2,1},{3,2},{4,3},{5,4},{6,5},{7,6},{8,7},{9,8},{10,9},{11,1... | collective-permute-start | bytes 6291464 | tf_op jit(solution)/shard_map/ppermute | solution.py:23
  432.2 28.1 %collective-permute-start.4 = (bf16[2,1,4,2,256,256]{4,5,3,2,0,1:T(8,128)(2,1)S(1)}, bf16[2,1,4,2,256,256]{4,5,3,2,0,1:T(8,128)(2,1)S(1)}, u32[]{:S(2)}, u32[]{:S(2)}) collective-permute-start(bf16[2,1,4,2,256,256]{4,5,3,2,0,1:T(8,128)(2,1)S(1)} %slice.49), channel_id=1, source_target_pairs={{0,1},{1,2},{2,3},{3,4},{4,5},{5,6},{6,7},{7,8},{8,9},{9,10},{10,1... | collective-permute-start | bytes 6291464 | tf_op jit(solution)/shard_map/ppermute | solution.py:22
  434.1 26.2 %collective-permute-start.5 = (bf16[1,1,5,256,256]{4,3,2,1,0:T(8,128)(2,1)S(1)}, bf16[1,1,5,256,256]{4,3,2,1,0:T(8,128)(2,1)S(1)}, u32[]{:S(2)}, u32[]{:S(2)}) collective-permute-start(bf16[1,1,5,256,256]{4,3,2,1,0:T(8,128)(2,1)S(1)} %copy-done.8), channel_id=1, source_target_pairs={{0,128},{128,0},{1,129},{129,1},{2,130},{130,2},{3,131},{131,3},{4... | collective-permute-start | bytes 1966088 | tf_op jit(solution)/shard_map/ppermute | solution.py:12
  460.3 3.3 copy-start.9
  463.6 690.7 %copy-start = (f32[2,4,256,256,1]{3,2,4,1,0:T(8,128)}, f32[2,4,256,256,1]{3,2,4,1,0:T(8,128)S(1)}, u32[]{:S(2)}) copy-start(f32[2,4,256,256,1]{3,2,4,1,0:T(8,128)S(1)} %get-tuple-element.134) | copy-start | bytes 6291460
  1213.4 28.1 %collective-permute-start.6 = (bf16[2,1,4,2,256,256]{4,5,3,2,0,1:T(8,128)(2,1)S(1)}, bf16[2,1,4,2,256,256]{4,5,3,2,0,1:T(8,128)(2,1)S(1)}, u32[]{:S(2)}, u32[]{:S(2)}) collective-permute-start(bf16[2,1,4,2,256,256]{4,5,3,2,0,1:T(8,128)(2,1)S(1)} %slice.53), channel_id=1, source_target_pairs={{1,0},{2,1},{3,2},{4,3},{5,4},{6,5},{7,6},{8,7},{9,8},{10,9},{11,1... | collective-permute-start | bytes 6291464 | tf_op jit(solution)/shard_map/ppermute | solution.py:23
  1215.5 28.1 %collective-permute-start.7 = (bf16[2,1,4,2,256,256]{4,5,3,2,0,1:T(8,128)(2,1)S(1)}, bf16[2,1,4,2,256,256]{4,5,3,2,0,1:T(8,128)(2,1)S(1)}, u32[]{:S(2)}, u32[]{:S(2)}) collective-permute-start(bf16[2,1,4,2,256,256]{4,5,3,2,0,1:T(8,128)(2,1)S(1)} %slice.53), channel_id=1, source_target_pairs={{0,1},{1,2},{2,3},{3,4},{4,5},{5,6},{6,7},{7,8},{8,9},{9,10},{10,1... | collective-permute-start | bytes 6291464 | tf_op jit(solution)/shard_map/ppermute | solution.py:22
  1221.4 22.3 %copy-start.10 = (bf16[1,1,5,256,256]{4,3,2,1,0:T(8,128)(2,1)S(1)}, bf16[1,1,5,256,256]{4,3,2,1,0:T(8,128)(2,1)}, u32[]{:S(2)}) copy-start(bf16[1,1,5,256,256]{4,3,2,1,0:T(8,128)(2,1)} %copy-done.9) | copy-start | bytes 1966084
  1243.8 346.3 %copy-start.1 = (f32[2,4,256,256,1]{3,2,4,1,0:T(8,128)S(1)}, f32[2,4,256,256,1]{3,2,4,1,0:T(8,128)}, u32[]{:S(2)}) copy-start(f32[2,4,256,256,1]{3,2,4,1,0:T(8,128)} %copy-done) | copy-start | bytes 6291460
  1590.0 5.0 copy-start.4
  1595.0 3.0 copy-start.2
where the time goes:
time: 1620 us; the launch traced here: 1600 us
  blocking collectives  1370 us (85%)
  matrix products  80.6 us (5%)
  local copies, waits for them, and re-layouts  54.5 us (3%)
  waiting for transfers between devices  52.4 us (3%)
  starting transfers between devices  23.2 us (1%)
    psum x1, blocking collectives, body(): start_sq = lax.psum(totals(start_f * start_f), 'sec')  347 us
    psum x1, blocking collectives, body(): residual_sq = lax.psum(totals(residual_v * residual_v), 'sec')  345 us
    psum x1, blocking collectives, body(): rayleigh = lax.psum(totals(vector_v * image_v), 'sec')  342 us
    psum x1, blocking collectives, body(): lax.psum((totals(vector_v * image_u), totals(second_v * image_u)), 'sec')  342 us
    dot_general x4, matrix products, one_vector(): jnp.einsum('wxts,qsxac->qtwac', mpo_kept, stacked, precision=lax.Precisio...  58.4 us
    ppermute x3, waiting for transfers between devices, padded_2(): after = lax.ppermute(leading, axis, down)  41.5 us
  transfers between devices with their start and end apart: 8, of which 6 were waited for; matrix products, arithmetic and copies ran while one was open for 0% of the time, Pallas kernels for 0%

commit v1 on v0

v1 whole, which is shorter than its diff:
```python
import jax
import jax.numpy as jnp
from jax import lax
from jax.experimental import pallas as pl
from jax.experimental.pallas import tpu as pltpu
from jax.sharding import PartitionSpec as P

MESH = pl.DeviceIdType.MESH
F32 = jnp.float32
BF16 = jnp.bfloat16
EPSILON = 1e-06
CHARGE = (0, 1, 1, 2)
SHIFT = (0, 0, 0, 1, -1)
SLOT_OF = {0: 0, 3: 1, 1: 2, 2: 3}
SPIN_OF = (0, 3, 1, 2)


def couplings(spin, channel, spin_in):
    change = CHARGE[spin] - CHARGE[spin_in]
    return [w2 for w2 in range(5) if change == SHIFT[channel] - SHIFT[w2]]


COEFS = [
    (w2, spin, channel, spin_in)
    for spin in range(4)
    for channel in range(5)
    for spin_in in range(4)
    for w2 in couplings(spin, channel, spin_in)
]
COEF_AT = {key: index for index, key in enumerate(COEFS)}


def grid_sizes(count):
    return {128: (4, 4, 8), 8: (2, 2, 2)}[count]


def folded(value):
    rows, columns = value.shape
    value = value.reshape(rows // 8, 8, columns).sum(axis=0)
    total = value[:, :128]
    for start in range(128, columns, 128):
        total = total + value[:, start : start + 128]
    return total


def whole(value):
    return jnp.sum(jnp.sum(value, axis=1, keepdims=True), axis=0, keepdims=True)


def kernel(
    sizes,
    mpo_ref,
    start_ref,
    left_ref,
    right_ref,
    vector_ref,
    residual_ref,
    energy_ref,
    us,
    xs,
    part,
    right_buf,
    left_buf,
    blended,
    send_buf,
    recv_buf,
    hs,
    out_buf,
    ar_x,
    ar_y,
    ar_z,
    kept,
    coef,
    in_sem,
    r_send,
    r_recv,
    l_send,
    l_recv,
    b_send,
    b_recv,
    ar_send,
    ar_recv,
    out_sem,
):
    size_x, size_y, size_z = sizes
    count = size_x * size_y * size_z
    block = start_ref.shape[-1]
    step_rows = 32
    sect = lax.axis_index("sect")
    sec = lax.axis_index("sec")
    other = 1 - sect
    up = lax.rem(sec + 1, count)
    down = lax.rem(sec + count - 1, count)
    at_x = lax.rem(sec, size_x)
    at_y = lax.rem(sec // size_x, size_y)
    at_z = sec // (size_x * size_y)

    def partner_x(k):
        there = lax.rem(at_x + k, size_x)
        return there, sec - at_x + there

    def partner_y(k):
        there = lax.rem(at_y + k, size_y)
        return there, sec + (there - at_y) * size_x

    def partner_z(k):
        there = lax.rem(at_z + k, size_z)
        return there, sec + (there - at_z) * (size_x * size_y)

    def device(section, sector):
        return {"sect": section, "sec": sector}

    def remote(source, target, send_sem, recv_sem, where):
        return pltpu.make_async_remote_copy(
            src_ref=source,
            dst_ref=target,
            send_sem=send_sem,
            recv_sem=recv_sem,
            device_id=where,
            device_id_type=MESH,
        )

    loads = [
        pltpu.make_async_copy(start_ref.at[0, v, 0], us.at[v], in_sem.at[v]) for v in range(2)
    ]
    for load in loads:
        load.start()

    barrier = pltpu.get_barrier_semaphore()
    greeted = [device(other, sec), device(other, up), device(other, down)]
    greeted += [device(sect, up), device(sect, down)]
    greeted += [device(sect, partner_x(k)[1]) for k in range(1, size_x)]
    greeted += [device(sect, partner_y(k)[1]) for k in range(1, size_y)]
    greeted += [device(sect, partner_z(k)[1]) for k in range(1, size_z)]
    for where in greeted:
        pl.semaphore_signal(barrier, inc=1, device_id=where, device_id_type=MESH)
    pl.semaphore_wait(barrier, len(greeted))

    def right_copy(slot, part):
        first, last = ((3, 5), (0, 3))[part]
        return remote(
            right_ref.at[0, 0, first:last],
            right_buf.at[slot, first:last],
            r_send.at[slot, part],
            r_recv.at[slot, part],
            device(other, (up, sec, down)[slot]),
        )

    def left_copy(channel):
        return remote(
            left_ref.at[0, 0, channel],
            left_buf.at[:, channel * block : (channel + 1) * block],
            l_send.at[channel],
            l_recv.at[channel],
            device(other, sec),
        )

    right_copies = [right_copy(*k) for k in ((0, 0), (2, 0), (1, 0), (1, 1), (0, 1), (2, 1))]
    left_copies = [left_copy(channel) for channel in range(5)]
    for copy in right_copies + left_copies:
        copy.start()

    for (w2, spin, channel, spin_in), index in COEF_AT.items():
        there = sec + (CHARGE[spin_in] - 1)
        origin = there - SHIFT[w2]
        keep = (there >= 0) & (there < count) & (origin >= 0) & (origin < count)
        coef[index] = mpo_ref[channel, w2, spin, spin_in] * jnp.where(keep, 1.0, 0.0).astype(F32)

    def multiply(phase, v, spins, channels):
        low, high = spins
        first, last = channels
        right = right_buf[CHARGE[low], first:last].reshape((last - first) * block, block)
        vectors = xs[phase, low:high].reshape((high - low) * block, block)
        product = lax.dot_general(
            vectors, right, (((1,), (1,)), ((), ())), preferred_element_type=F32
        )
        for spin_in in range(low, high):
            for w2 in range(first, last):
                part[v, spin_in, w2] = product[
                    (spin_in - low) * block : (spin_in - low + 1) * block,
                    (w2 - first) * block : (w2 - first + 1) * block,
                ]

    def multiply_all(phase, v):
        multiply(phase, v, (1, 3), (0, 5))
        multiply(phase, v, (0, 1), (0, 5))
        multiply(phase, v, (3, 4), (0, 5))

    def mix(v, targets, store):
        def step(i, carry):
            rows = pl.ds(pl.multiple_of(i * 16, 16), 16)
            held = {}
            for spin, channel in targets:
                total = None
                for spin_in in range(4):
                    for w2 in couplings(spin, channel, spin_in):
                        key = (spin_in, w2)
                        if key not in held:
                            held[key] = part[v, spin_in, w2, rows, :]
                        term = coef[COEF_AT[(w2, spin, channel, spin_in)]] * held[key]
                        total = term if total is None else total + term
                store(spin, channel, rows, i, total.astype(BF16))
            return carry

        lax.fori_loop(0, block // 16, step, 0)

    def block_copy(phase, side, half):
        return remote(
            send_buf.at[phase, side, 2 * half : 2 * half + 2],
            recv_buf.at[phase, 2 * half : 2 * half + 2, side * block : (side + 1) * block],
            b_send.at[phase, side, half],
            b_recv.at[phase, side, half],
            device(sect, (down, up)[side]),
        )

    def produce(phase, v, half):
        def store(spin, channel, rows, i, value):
            send_buf[phase, channel - 3, SLOT_OF[spin], rows, :] = value

        mix(v, [(spin, w) for spin in ((0, 3), (1, 2))[half] for w in (3, 4)], store)
        for side in range(2):
            block_copy(phase, side, half).start()

    def local(phase, v):
        def store(spin, channel, rows, i, value):
            start = pl.multiple_of(channel * block + i * 16, 16)
            blended[spin, pl.ds(start, 16), :] = value

        for channel in range(3):
            mix(v, [(spin, channel) for spin in range(4)], store)
        for spin in range(4):
            hs[phase, spin] = jnp.dot(
                left_buf[:, : 3 * block], blended[spin], preferred_element_type=F32
            )

    def consume(phase):
        for half in range(2):
            for side in range(2):
                block_copy(phase, side, half).wait_recv()
            for slot in (2 * half, 2 * half + 1):
                spin = SPIN_OF[slot]
                hs[phase, spin] += jnp.dot(
                    left_buf[:, 3 * block :],
                    recv_buf[phase, slot],
                    preferred_element_type=F32,
                )

    def over_rows(function, init):
        total = init
        for spin in range(4):

            def step(i, carry, spin=spin):
                rows = pl.ds(pl.multiple_of(i * step_rows, step_rows), step_rows)
                return function(spin, rows, carry)

            total = lax.fori_loop(0, block // step_rows, step, total)
        return total

    zero = jnp.zeros((8, 128), F32)

    def all_reduce(phase, values):
        for index, value in enumerate(values):
            ar_x[phase, at_x, index] = value
        stages = (
            (ar_x, at_x, size_x, partner_x, 0),
            (ar_y, at_y, size_y, partner_y, size_x - 1),
            (ar_z, at_z, size_z, partner_z, size_x + size_y - 2),
        )
        for number, (held, at, size, partner, base) in enumerate(stages):
            copies = []
            arrivals = []
            for k in range(1, size):
                there, sector = partner(k)
                copies.append(
                    remote(
                        held.at[phase, at],
                        held.at[phase, at],
                        ar_send.at[phase, base + k - 1],
                        ar_recv.at[phase, number, at],
                        device(sect, sector),
                    )
                )
                arrivals.append(
                    remote(
                        held.at[phase, there],
                        held.at[phase, there],
                        ar_send.at[phase, base + k - 1],
                        ar_recv.at[phase, number, there],
                        device(sect, sector),
                    )
                )
            for copy in copies:
                copy.start()
            for arrival in arrivals:
                arrival.wait_recv()
            totals = held[phase, 0]
            for index in range(1, size):
                totals = totals + held[phase, index]
            for copy in copies:
                copy.wait_send()
            if number < 2:
                following, place = stages[number + 1][:2]
                following[phase, place] = totals
        return [whole(totals[index]) for index in range(3)]

    def start_block(v, spin, rows):
        value = us[v, spin, rows, :].astype(F32)
        if spin == 0:
            value = value * jnp.where(sec == 0, 0.0, 1.0).astype(F32)
        if spin == 3:
            value = value * jnp.where(sec == count - 1, 0.0, 1.0).astype(F32)
        return value

    def start_sum(v):
        def step(spin, rows, carry):
            value = start_block(v, spin, rows)
            return carry + folded(value * value)

        return over_rows(step, zero)

    def make_first(v, start_sq):
        inv_norm = 1.0 / jnp.sqrt(start_sq + EPSILON)

        def step(spin, rows, carry):
            xs[v, spin, rows, :] = (start_block(v, spin, rows) * inv_norm).astype(BF16)
            return carry

        over_rows(step, 0)

    def first_sums(v):
        def step(spin, rows, carry):
            squared, product, image_sq = carry
            x = xs[v, spin, rows, :].astype(F32)
            image = hs[v, spin, rows, :]
            return (
                squared + folded(x * x),
                product + folded(x * image),
                image_sq + folded(image * image),
            )

        return over_rows(step, (zero, zero, zero))

    def make_second(v, squared, rayleigh, image_sq):
        estimate = image_sq - 2.0 * rayleigh * rayleigh + rayleigh * rayleigh * squared
        norm = jnp.sqrt(jnp.maximum(estimate, 0.0) + EPSILON)
        inv_norm = 1.0 / norm

        def step(spin, rows, carry):
            x = xs[v, spin, rows, :].astype(F32)
            value = hs[v, spin, rows, :] - rayleigh * x
            xs[v + 2, spin, rows, :] = (value * inv_norm).astype(BF16)
            return carry + folded(value * value)

        kept[v, 0] = jnp.broadcast_to(rayleigh, (8, 128))
        kept[v, 1] = jnp.broadcast_to(norm, (8, 128))
        kept[v, 2] = over_rows(step, zero)

    def second_sums(v):
        def step(spin, rows, carry):
            mixed, diagonal = carry
            x = xs[v, spin, rows, :].astype(F32)
            image = hs[v + 2, spin, rows, :]
            second = xs[v + 2, spin, rows, :].astype(F32)
            return mixed + folded(x * image), diagonal + folded(second * image)

        return over_rows(step, (zero, zero))

    def out_copies(v, spin):
        return [
            pltpu.make_async_copy(
                out_buf.at[which, v, spin], target.at[0, v, 0, spin], out_sem.at[which, v, spin]
            )
            for which, target in enumerate((vector_ref, residual_ref))
        ]

    def finish(v, residual_sq, coupling_raw, diagonal_raw):
        rayleigh = kept[v, 0, 0:1, 0:1]
        scale = kept[v, 1, 0:1, 0:1] / jnp.sqrt(residual_sq + EPSILON)
        coupling = coupling_raw * scale
        second_diag = diagonal_raw * scale * scale
        half_gap = 0.5 * (second_diag - rayleigh)
        radius = jnp.sqrt(half_gap * half_gap + coupling * coupling)
        energy = 0.5 * (rayleigh + second_diag) - radius
        flat = radius <= 0.0
        safe = jnp.where(flat, 1.0, radius)
        larger = jnp.sqrt(0.5 * (1.0 + jnp.abs(half_gap) / safe))
        smaller = 0.5 * jnp.abs(coupling) / (safe * larger)
        ahead = half_gap >= 0.0
        sign = jnp.where(coupling < 0.0, -1.0, 1.0)
        cosine = jnp.where(flat, 1.0, jnp.where(ahead, larger, smaller))
        sine = jnp.where(flat, 0.0, sign * jnp.where(ahead, smaller, larger))
        from_second = -sine * scale

        for spin in range(4):

            def step(i, carry, spin=spin):
                rows = pl.ds(pl.multiple_of(i * step_rows, step_rows), step_rows)
                x = xs[v, spin, rows, :].astype(F32)
                second = xs[v + 2, spin, rows, :].astype(F32)
                ritz = cosine * x + from_second * second
                out_buf[0, v, spin, rows, :] = ritz
                out_buf[1, v, spin, rows, :] = (
                    cosine * hs[v, spin, rows, :]
                    + from_second * hs[v + 2, spin, rows, :]
                    - energy * ritz
                )
                return carry

            lax.fori_loop(0, block // step_rows, step, 0)
            for copy in out_copies(v, spin):
                copy.start()
        energy_ref[0, v] = energy[0, 0]

    for load in loads:
        load.wait()
    for v, total in enumerate(all_reduce(0, (start_sum(0), start_sum(1), zero))[:2]):
        make_first(v, total)
    right_copy(1, 0).wait_recv()
    right_copy(1, 1).wait_recv()
    multiply(0, 0, (1, 3), (0, 5))
    right_copy(0, 0).wait_recv()
    right_copy(2, 0).wait_recv()
    multiply(0, 0, (0, 1), (3, 5))
    multiply(0, 0, (3, 4), (3, 5))
    produce(0, 0, 0)
    right_copy(0, 1).wait_recv()
    right_copy(2, 1).wait_recv()
    multiply(0, 0, (0, 1), (0, 3))
    multiply(0, 0, (3, 4), (0, 3))
    produce(0, 0, 1)
    multiply_all(1, 1)
    produce(1, 1, 0)
    produce(1, 1, 1)
    for copy in left_copies:
        copy.wait_recv()

    @pl.when(sec == count - 1)
    def _():
        left_buf[:, 3 * block : 4 * block] = jnp.zeros((block, block), BF16)

    @pl.when(sec == 0)
    def _():
        left_buf[:, 4 * block :] = jnp.zeros((block, block), BF16)

    def local_step(v, carry):
        local(v, v)
        return carry

    lax.fori_loop(0, 2, local_step, 0)

    def first_step(v, carry):
        consume(v)
        make_second(v, *all_reduce(v + 1, first_sums(v)))
        multiply_all(v + 2, v)
        produce(v + 2, v, 0)
        produce(v + 2, v, 1)
        local(v + 2, v)
        return carry

    lax.fori_loop(0, 2, first_step, 0)

    def second_step(v, carry):
        consume(v + 2)
        mixed, diagonal = second_sums(v)
        finish(v, *all_reduce(v + 3, (kept[v, 2], mixed, diagonal)))
        return carry

    lax.fori_loop(0, 2, second_step, 0)

    for copy in right_copies + left_copies:
        copy.wait_send()
    for phase in range(4):
        for side in range(2):
            for half in range(2):
                block_copy(phase, side, half).wait_send()
    for v in range(2):
        for spin in range(4):
            for copy in out_copies(v, spin):
                copy.wait()


def body(start_vectors, left_env, right_env, pair_mpo):
    block = start_vectors.shape[-1]
    count = lax.axis_size("sec")
    sizes = grid_sizes(count)
    partners = sum(sizes) - 3
    wide = (1, 2, 1, 4, block, block)
    any_spec = pl.BlockSpec(memory_space=pl.ANY)
    smem_spec = pl.BlockSpec(memory_space=pltpu.SMEM)
    dma = pltpu.SemaphoreType.DMA
    return pl.pallas_call(
        lambda *refs: kernel(sizes, *refs),
        name="davidson",
        out_shape=(
            jax.ShapeDtypeStruct(wide, F32),
            jax.ShapeDtypeStruct(wide, F32),
            jax.ShapeDtypeStruct((1, 2), F32),
        ),
        in_specs=[smem_spec, any_spec, any_spec, any_spec],
        out_specs=(any_spec, any_spec, smem_spec),
        scratch_shapes=[
            pltpu.VMEM((2, 4, block, block), BF16),
            pltpu.VMEM((4, 4, block, block), BF16),
            pltpu.VMEM((2, 4, 5, block, block), F32),
            pltpu.VMEM((3, 5, block, block), BF16),
            pltpu.VMEM((block, 5 * block), BF16),
            pltpu.VMEM((4, 3 * block, block), BF16),
            pltpu.VMEM((4, 2, 4, block, block), BF16),
            pltpu.VMEM((4, 4, 2 * block, block), BF16),
            pltpu.VMEM((4, 4, block, block), F32),
            pltpu.VMEM((2, 2, 4, block, block), F32),
            pltpu.VMEM((5, sizes[0], 3, 8, 128), F32),
            pltpu.VMEM((5, sizes[1], 3, 8, 128), F32),
            pltpu.VMEM((5, sizes[2], 3, 8, 128), F32),
            pltpu.VMEM((2, 3, 8, 128), F32),
            pltpu.SMEM((len(COEFS),), F32),
            dma((2,)),
            dma((3, 2)),
            dma((3, 2)),
            dma((5,)),
            dma((5,)),
            dma((4, 2, 2)),
            dma((4, 2, 2)),
            dma((5, partners)),
            dma((5, 3, max(sizes))),
            dma((2, 2, 4)),
        ],
        compiler_params=pltpu.CompilerParams(
            collective_id=0, has_side_effects=True, vmem_limit_bytes=56 * 1024 * 1024
        ),
    )(pair_mpo, start_vectors, left_env, right_env)


def solution(mesh):
    in_specs = (
        P("sect", None, "sec", None, None, None),
        P("sect", "sec", None, None, None),
        P("sect", "sec", None, None, None),
        P(),
    )
    out_specs = (
        P("sect", None, "sec", None, None, None),
        P("sect", None, "sec", None, None, None),
        P("sect", None),
    )
    return jax.shard_map(body, mesh=mesh, in_specs=in_specs, out_specs=out_specs, check_vma=False)
```

time: 1620 us -> 145 us (0.09); the launches traced: 1600 us -> 144 us
  blocking collectives: 1370 us -> 0 us
  Pallas kernels: 0 us -> 137 us
  matrix products: 80.6 us -> 0 us
  waiting for transfers between devices: 52.4 us -> 0 us
  local copies, waits for them, and re-layouts: 54.5 us -> 6.65 us
  starting transfers between devices: 23.2 us -> 0 us
    psum x4 -> x0, blocking collectives: 1370 us -> none  [the longest x1 347 us: body(): start_sq = lax.psum(totals(start_f * start_f), 'sec')]
    pallas_call x0 -> x1, Pallas kernels: none -> 137 us  [body(): pl.pallas_call(lambda *refs: kernel(sizes, *refs), name='davidson', out_s...]
    dot_general x22 -> x0, matrix products: 80.6 us -> none  [the longest x4 58.4 us: one_vector(): jnp.einsum('wxts,qsxac->qtwac', mpo_kept, stacked, precision=lax.Precisio...]
    ppermute x8 -> x0, waiting for transfers between devices: 52.4 us -> none  [the longest x3 41.5 us: padded_2(): after = lax.ppermute(leading, axis, down)]
    dynamic_update_slice x8 -> x0, local copies, waits for them, and re-layouts: 28.8 us -> none  [effective_apply(): blended = lax.map(one_vector, vector_b)]
    ppermute x8 -> x0, starting transfers between devices: 23.2 us -> none  [the longest x3 14.2 us: padded_2(): after = lax.ppermute(leading, axis, down)]
  transfers between devices with their start and end apart: 8 -> 0, of which waited for: 6 -> 0; matrix products, arithmetic and copies ran while one was open for 0% -> 0% of each run, Pallas kernels for 0% -> 0%
where the time goes in v1:
time: 145 us; the launch traced here: 144 us
  Pallas kernels  137 us (94%)
  local copies, waits for them, and re-layouts  6.65 us (5%)
    pallas_call x1, Pallas kernels, body(): pl.pallas_call(lambda *refs: kernel(sizes, *refs), name='davidson', out_s...  137 us
    unnamed x8, local copies, waits for them, and re-layouts  6.65 us

profile of v1, /device:TPU:2, one launch (start us, length us, event | category | flops | bytes accessed | tf_op | source)
XLA Modules:
  0.0 144.2 jit_solution(18215313656234014086)
XLA Ops:
  0.6 1.6 %copy.7.refs_0_ = f32[5,5,4,4]{3,2,1,0:T(4,128)} copy(f32[5,5,4,4]{1,3,2,0:T(4,128)} %param.7) | data formatting | bytes 3200 | tf_op args[3]
  2.3 136.9 %davidson.1 = (f32[1,2,1,4,256,256]{5,4,3,2,1,0:T(8,128)}, f32[1,2,1,4,256,256]{5,4,3,2,1,0:T(8,128)}, f32[1,2]{1,0:T(1,128)}) custom-call(f32[5,5,4,4]{3,2,1,0:T(4,128)} %copy.7.refs_0_, bf16[1,2,1,4,256,256]{5,4,3,2,1,0:T(8,128)(2,1)} %refs_1_.1, bf16[1,1,5,256,256]{4,3,2,1,0:T(8,128)(2,1)} %refs_2_.1, bf16[1,1,5,256,256]{4,3,2,1,0:T(8,128)(2,1)} %refs_3_.1), custom_call_target="tpu_custom_call" | custom-call | tf_op jit(solution)/shard_map/davidson/pallas_call | solution.py:491
  139.2 0.0 copy-start
  139.2 3.2 %copy.11 = f32[1,2,1,4,256,256]{5,4,3,2,1,0:T(8,128)} copy(f32[1,2,1,4,256,256]{5,4,3,2,1,0:T(8,128)} %get-tuple-element.6) | data formatting | bytes 4194304
  142.4 0.0 copy-done
  142.4 0.0 copy-start.1
  142.4 1.3 copy.12
  143.7 0.0 copy-done.1
  143.7 0.5 copy.13
Async XLA Ops:
  139.2 3.2 %copy-start = (f32[1,2,1,4,256,256]{5,4,3,2,1,0:T(8,128)S(1)}, f32[1,2,1,4,256,256]{5,4,3,2,1,0:T(8,128)}, u32[]{:S(2)}) copy-start(f32[1,2,1,4,256,256]{5,4,3,2,1,0:T(8,128)} %get-tuple-element.7) | copy-start | bytes 6291460
  142.4 1.3 copy-start.1

commit v2 on v1

--- a/solution.py
+++ b/solution.py
@@ -31,7 +31,11 @@
 
 
 def grid_sizes(count):
-    return {128: (4, 4, 8), 8: (2, 2, 2)}[count]
+    return {128: (16, 8), 8: (4, 2)}[count]
+
+
+def folded_rows(value):
+    return jnp.sum(value, axis=0, keepdims=True)
 
 
 def folded(value):
@@ -66,9 +70,6 @@
     recv_buf,
     hs,
     out_buf,
-    ar_x,
-    ar_y,
-    ar_z,
     kept,
     coef,
     in_sem,
@@ -81,9 +82,11 @@
     ar_send,
     ar_recv,
     out_sem,
+    *sums,
 ):
-    size_x, size_y, size_z = sizes
-    count = size_x * size_y * size_z
+    count = 1
+    for size in sizes:
+        count *= size
     block = start_ref.shape[-1]
     step_rows = 32
     sect = lax.axis_index("sect")
@@ -91,21 +94,16 @@
     other = 1 - sect
     up = lax.rem(sec + 1, count)
     down = lax.rem(sec + count - 1, count)
-    at_x = lax.rem(sec, size_x)
-    at_y = lax.rem(sec // size_x, size_y)
-    at_z = sec // (size_x * size_y)
-
-    def partner_x(k):
-        there = lax.rem(at_x + k, size_x)
-        return there, sec - at_x + there
-
-    def partner_y(k):
-        there = lax.rem(at_y + k, size_y)
-        return there, sec + (there - at_y) * size_x
-
-    def partner_z(k):
-        there = lax.rem(at_z + k, size_z)
-        return there, sec + (there - at_z) * (size_x * size_y)
+    stages = []
+    stride = 1
+    for size in sizes:
+        stages.append((size, stride, lax.rem(sec // stride, size)))
+        stride *= size
+
+    def partner(stage, k):
+        size, stride, digit = stages[stage]
+        there = lax.rem(digit + k, size)
+        return there, sec + (there - digit) * stride
 
     def device(section, sector):
         return {"sect": section, "sec": sector}
@@ -120,21 +118,19 @@
             device_id_type=MESH,
         )
 
+    barrier = pltpu.get_barrier_semaphore()
+    greeted = [device(other, sec), device(other, up), device(other, down)]
+    greeted += [device(sect, up), device(sect, down)]
+    for stage, size in enumerate(sizes):
+        greeted += [device(sect, partner(stage, k)[1]) for k in range(1, size)]
+    for where in greeted:
+        pl.semaphore_signal(barrier, inc=1, device_id=where, device_id_type=MESH)
     loads = [
         pltpu.make_async_copy(start_ref.at[0, v, 0], us.at[v], in_sem.at[v]) for v in range(2)
     ]
     for load in loads:
         load.start()
 
-    barrier = pltpu.get_barrier_semaphore()
-    greeted = [device(other, sec), device(other, up), device(other, down)]
-    greeted += [device(sect, up), device(sect, down)]
-    greeted += [device(sect, partner_x(k)[1]) for k in range(1, size_x)]
-    greeted += [device(sect, partner_y(k)[1]) for k in range(1, size_y)]
-    greeted += [device(sect, partner_z(k)[1]) for k in range(1, size_z)]
-    for where in greeted:
-        pl.semaphore_signal(barrier, inc=1, device_id=where, device_id_type=MESH)
-    pl.semaphore_wait(barrier, len(greeted))
 
     def right_copy(slot, part):
         first, last = ((3, 5), (0, 3))[part]
@@ -157,14 +153,6 @@
 
     right_copies = [right_copy(*k) for k in ((0, 0), (2, 0), (1, 0), (1, 1), (0, 1), (2, 1))]
     left_copies = [left_copy(channel) for channel in range(5)]
-    for copy in right_copies + left_copies:
-        copy.start()
-
-    for (w2, spin, channel, spin_in), index in COEF_AT.items():
-        there = sec + (CHARGE[spin_in] - 1)
-        origin = there - SHIFT[w2]
-        keep = (there >= 0) & (there < count) & (origin >= 0) & (origin < count)
-        coef[index] = mpo_ref[channel, w2, spin, spin_in] * jnp.where(keep, 1.0, 0.0).astype(F32)
 
     def multiply(phase, v, spins, channels):
         low, high = spins
@@ -218,8 +206,15 @@
             send_buf[phase, channel - 3, SLOT_OF[spin], rows, :] = value
 
         mix(v, [(spin, w) for spin in ((0, 3), (1, 2))[half] for w in (3, 4)], store)
+
+    def send(phase, half):
         for side in range(2):
             block_copy(phase, side, half).start()
+
+    def sent(phase):
+        for half in range(2):
+            for side in range(2):
+                block_copy(phase, side, half).wait_send()
 
     def local(phase, v):
         def store(spin, channel, rows, i, value):
@@ -258,50 +253,58 @@
 
     zero = jnp.zeros((8, 128), F32)
 
-    def all_reduce(phase, values):
-        for index, value in enumerate(values):
-            ar_x[phase, at_x, index] = value
-        stages = (
-            (ar_x, at_x, size_x, partner_x, 0),
-            (ar_y, at_y, size_y, partner_y, size_x - 1),
-            (ar_z, at_z, size_z, partner_z, size_x + size_y - 2),
-        )
-        for number, (held, at, size, partner, base) in enumerate(stages):
-            copies = []
-            arrivals = []
-            for k in range(1, size):
-                there, sector = partner(k)
-                copies.append(
-                    remote(
-                        held.at[phase, at],
-                        held.at[phase, at],
-                        ar_send.at[phase, base + k - 1],
-                        ar_recv.at[phase, number, at],
-                        device(sect, sector),
-                    )
-                )
-                arrivals.append(
-                    remote(
-                        held.at[phase, there],
-                        held.at[phase, there],
-                        ar_send.at[phase, base + k - 1],
-                        ar_recv.at[phase, number, there],
-                        device(sect, sector),
-                    )
-                )
-            for copy in copies:
-                copy.start()
-            for arrival in arrivals:
-                arrival.wait_recv()
-            totals = held[phase, 0]
-            for index in range(1, size):
-                totals = totals + held[phase, index]
-            for copy in copies:
-                copy.wait_send()
-            if number < 2:
-                following, place = stages[number + 1][:2]
-                following[phase, place] = totals
-        return [whole(totals[index]) for index in range(3)]
+    def sum_copies(phase):
+        def copy_to(stage, k):
+            digit = stages[stage][2]
+            return remote(
+                sums[stage].at[phase, digit],
+                sums[stage].at[phase, digit],
+                ar_send.at[phase, stage, k],
+                ar_recv.at[phase, stage, digit],
+                device(sect, partner(stage, k)[1]),
+            )
+
+        def copy_from(stage, k):
+            there, sector = partner(stage, k)
+            return remote(
+                sums[stage].at[phase, there],
+                sums[stage].at[phase, there],
+                ar_send.at[phase, stage, k],
+                ar_recv.at[phase, stage, there],
+                device(sect, sector),
+            )
+
+        return copy_to, copy_from
+
+    def send_sums(phase, stage, total):
+        copy_to, _ = sum_copies(phase)
+        size, _, digit = stages[stage]
+        sums[stage][phase, digit] = total
+        for k in range(1, size):
+            copy_to(stage, k).start()
+
+    def take_sums(phase, stage):
+        _, copy_from = sum_copies(phase)
+        size = sizes[stage]
+        for k in range(1, size):
+            copy_from(stage, k).wait_recv()
+        total = sums[stage][phase, 0]
+        for index in range(1, size):
+            total = total + sums[stage][phase, index]
+        return total
+
+    def begin_sum(phase, values):
+        rows = [folded_rows(value) for value in values]
+        rows.append(jnp.zeros((8 - len(rows), 128), F32))
+        send_sums(phase, 0, jnp.concatenate(rows, axis=0))
+
+    def pass_sum(phase):
+        for stage in range(1, len(sizes)):
+            send_sums(phase, stage, take_sums(phase, stage - 1))
+
+    def end_sum(phase):
+        total = jnp.sum(take_sums(phase, len(sizes) - 1), axis=1, keepdims=True)
+        return [total[k : k + 1, :] for k in range(3)]
 
     def start_block(v, spin, rows):
         value = us[v, spin, rows, :].astype(F32)
@@ -413,10 +416,23 @@
 
     for load in loads:
         load.wait()
-    for v, total in enumerate(all_reduce(0, (start_sum(0), start_sum(1), zero))[:2]):
-        make_first(v, total)
+    start_sq = [start_sum(v) for v in range(2)]
+    pl.semaphore_wait(barrier, len(greeted))
+    begin_sum(0, start_sq)
+    for copy in right_copies + left_copies:
+        copy.start()
+    for (w2, spin, channel, spin_in), index in COEF_AT.items():
+        there = sec + (CHARGE[spin_in] - 1)
+        origin = there - SHIFT[w2]
+        keep = (there >= 0) & (there < count) & (origin >= 0) & (origin < count)
+        coef[index] = mpo_ref[channel, spin][spin_in, w2] * jnp.where(keep, 1.0, 0.0).astype(F32)
+
+    pass_sum(0)
     right_copy(1, 0).wait_recv()
     right_copy(1, 1).wait_recv()
+    start_sq = end_sum(0)
+    make_first(0, start_sq[0])
+
     multiply(0, 0, (1, 3), (0, 5))
     right_copy(0, 0).wait_recv()
     right_copy(2, 0).wait_recv()
@@ -425,9 +441,12 @@
     produce(0, 0, 0)
     right_copy(0, 1).wait_recv()
     right_copy(2, 1).wait_recv()
+    send(0, 0)
     multiply(0, 0, (0, 1), (0, 3))
     multiply(0, 0, (3, 4), (0, 3))
     produce(0, 0, 1)
+    send(0, 1)
+    make_first(1, start_sq[1])
     multiply_all(1, 1)
     produce(1, 1, 0)
     produce(1, 1, 1)
@@ -442,37 +461,55 @@
     def _():
         left_buf[:, 4 * block :] = jnp.zeros((block, block), BF16)
 
-    def local_step(v, carry):
-        local(v, v)
-        return carry
-
-    lax.fori_loop(0, 2, local_step, 0)
-
-    def first_step(v, carry):
-        consume(v)
-        make_second(v, *all_reduce(v + 1, first_sums(v)))
-        multiply_all(v + 2, v)
-        produce(v + 2, v, 0)
-        produce(v + 2, v, 1)
-        local(v + 2, v)
-        return carry
-
-    lax.fori_loop(0, 2, first_step, 0)
-
-    def second_step(v, carry):
-        consume(v + 2)
-        mixed, diagonal = second_sums(v)
-        finish(v, *all_reduce(v + 3, (kept[v, 2], mixed, diagonal)))
-        return carry
-
-    lax.fori_loop(0, 2, second_step, 0)
-
+    local(0, 0)
+    sent(0)
+    send(1, 0)
+    send(1, 1)
+    consume(0)
+    begin_sum(1, first_sums(0))
+    local(1, 1)
+    pass_sum(1)
+    make_second(0, *end_sum(1))
+
+    multiply_all(2, 0)
+    produce(2, 0, 0)
+    sent(1)
+    send(2, 0)
+    produce(2, 0, 1)
+    send(2, 1)
+    consume(1)
+    begin_sum(2, first_sums(1))
+    local(2, 0)
+    pass_sum(2)
+    make_second(1, *end_sum(2))
+    multiply_all(3, 1)
+    produce(3, 1, 0)
+    sent(2)
+    send(3, 0)
+    produce(3, 1, 1)
+    send(3, 1)
+    consume(2)
+    begin_sum(3, (kept[0, 2], *second_sums(0)))
+    local(3, 1)
+    pass_sum(3)
+    finish(0, *end_sum(3))
+    consume(3)
+    begin_sum(4, (kept[1, 2], *second_sums(1)))
+    pass_sum(4)
+    finish(1, *end_sum(4))
+
+    sent(3)
     for copy in right_copies + left_copies:
         copy.wait_send()
-    for phase in range(4):
-        for side in range(2):
-            for half in range(2):
-                block_copy(phase, side, half).wait_send()
+
+    def sums_sent(phase, carry):
+        copy_to, _ = sum_copies(phase)
+        for stage, size in enumerate(sizes):
+            for k in range(1, size):
+                copy_to(stage, k).wait_send()
+        return carry
+
+    lax.fori_loop(0, 5, sums_sent, 0)
     for v in range(2):
         for spin in range(4):
             for copy in out_copies(v, spin):
@@ -483,9 +520,9 @@
     block = start_vectors.shape[-1]
     count = lax.axis_size("sec")
     sizes = grid_sizes(count)
-    partners = sum(sizes) - 3
     wide = (1, 2, 1, 4, block, block)
     any_spec = pl.BlockSpec(memory_space=pl.ANY)
+    vmem_spec = pl.BlockSpec(memory_space=pltpu.VMEM)
     smem_spec = pl.BlockSpec(memory_space=pltpu.SMEM)
     dma = pltpu.SemaphoreType.DMA
     return pl.pallas_call(
@@ -496,7 +533,7 @@
             jax.ShapeDtypeStruct(wide, F32),
             jax.ShapeDtypeStruct((1, 2), F32),
         ),
-        in_specs=[smem_spec, any_spec, any_spec, any_spec],
+        in_specs=[vmem_spec, any_spec, any_spec, any_spec],
         out_specs=(any_spec, any_spec, smem_spec),
         scratch_shapes=[
             pltpu.VMEM((2, 4, block, block), BF16),
@@ -509,9 +546,6 @@
             pltpu.VMEM((4, 4, 2 * block, block), BF16),
             pltpu.VMEM((4, 4, block, block), F32),
             pltpu.VMEM((2, 2, 4, block, block), F32),
-            pltpu.VMEM((5, sizes[0], 3, 8, 128), F32),
-            pltpu.VMEM((5, sizes[1], 3, 8, 128), F32),
-            pltpu.VMEM((5, sizes[2], 3, 8, 128), F32),
             pltpu.VMEM((2, 3, 8, 128), F32),
             pltpu.SMEM((len(COEFS),), F32),
             dma((2,)),
@@ -521,14 +555,15 @@
             dma((5,)),
             dma((4, 2, 2)),
             dma((4, 2, 2)),
-            dma((5, partners)),
-            dma((5, 3, max(sizes))),
+            dma((5, len(sizes), max(sizes))),
+            dma((5, len(sizes), max(sizes))),
             dma((2, 2, 4)),
+            *[pltpu.VMEM((5, size, 8, 128), F32) for size in sizes],
         ],
         compiler_params=pltpu.CompilerParams(
             collective_id=0, has_side_effects=True, vmem_limit_bytes=56 * 1024 * 1024
         ),
-    )(pair_mpo, start_vectors, left_env, right_env)
+    )(jnp.transpose(pair_mpo, (0, 2, 3, 1)), start_vectors, left_env, right_env)
 
 
 def solution(mesh):

time: 145 us -> 126 us (0.87)
  Pallas kernels: 137 us -> 120 us
  local copies, waits for them, and re-layouts: 6.65 us -> 5.03 us
    pallas_call x1, Pallas kernels: 137 us -> 120 us  [body(): pl.pallas_call(lambda *refs: kernel(sizes, *refs), name='davidson', out_s...]
    unnamed x8 -> x7, local copies, waits for them, and re-layouts: 6.65 us -> 5.03 us
where the time goes in v2:
time: 126 us
  Pallas kernels  120 us (95%)
  local copies, waits for them, and re-layouts  5.03 us (4%)
    pallas_call x1, Pallas kernels, body(): pl.pallas_call(lambda *refs: kernel(sizes, *refs), name='davidson', out_s...  120 us
    unnamed x7, local copies, waits for them, and re-layouts  5.03 us

profile of v2, /device:TPU:2, one launch (start us, length us, event | category | flops | bytes accessed | tf_op | source)
XLA Modules:
  0.0 125.8 jit_solution(1506577928683642606)
XLA Ops:
  0.6 120.1 %davidson.1 = (f32[1,2,1,4,256,256]{5,4,3,2,1,0:T(8,128)}, f32[1,2,1,4,256,256]{5,4,3,2,1,0:T(8,128)}, f32[1,2]{1,0:T(1,128)}) custom-call(f32[5,4,4,5]{3,2,1,0:T(4,128)} %bitcast.1, bf16[1,2,1,4,256,256]{5,4,3,2,1,0:T(8,128)(2,1)} %refs_1_.1, bf16[1,1,5,256,256]{4,3,2,1,0:T(8,128)(2,1)} %refs_2_.1, bf16[1,1,5,256,256]{4,3,2,1,0:T(8,128)(2,1)} %refs_3_.1), custom_call_target="tpu_custom_call" | custom-call | tf_op jit(solution)/shard_map/davidson/pallas_call | solution.py:528
  120.8 0.0 copy-start
  120.8 3.2 %copy.10 = f32[1,2,1,4,256,256]{5,4,3,2,1,0:T(8,128)} copy(f32[1,2,1,4,256,256]{5,4,3,2,1,0:T(8,128)} %get-tuple-element.6) | data formatting | bytes 4194304
  124.0 0.0 copy-done
  124.0 0.0 copy-start.1
  124.0 1.3 %copy.11 = f32[1,2,1,4,256,256]{5,4,3,2,1,0:T(8,128)} copy(f32[1,2,1,4,256,256]{5,4,3,2,1,0:T(8,128)S(1)} %copy-done) | data formatting | bytes 4194304
  125.3 0.0 copy-done.1
  125.3 0.5 copy.12
Async XLA Ops:
  120.8 3.2 %copy-start = (f32[1,2,1,4,256,256]{5,4,3,2,1,0:T(8,128)S(1)}, f32[1,2,1,4,256,256]{5,4,3,2,1,0:T(8,128)}, u32[]{:S(2)}) copy-start(f32[1,2,1,4,256,256]{5,4,3,2,1,0:T(8,128)} %get-tuple-element.7) | copy-start | bytes 6291460
  124.0 1.3 %copy-start.1 = (f32[1,2]{1,0:T(1,128)S(1)}, f32[1,2]{1,0:T(1,128)}, u32[]{:S(2)}) copy-start(f32[1,2]{1,0:T(1,128)} %get-tuple-element.8) | copy-start | bytes 28

commit v3 on v2

--- a/solution.py
+++ b/solution.py
@@ -100,10 +100,23 @@
         stages.append((size, stride, lax.rem(sec // stride, size)))
         stride *= size
 
+    partners = [
+        [
+            (lax.rem(digit + k, size), sec + (lax.rem(digit + k, size) - digit) * stride)
+            for k in range(size)
+        ]
+        for size, stride, digit in stages
+    ]
+
     def partner(stage, k):
-        size, stride, digit = stages[stage]
-        there = lax.rem(digit + k, size)
-        return there, sec + (there - digit) * stride
+        return partners[stage][k]
+
+    def far_first(size):
+        inner = 4 if size == 16 else size
+        return sorted(
+            range(1, size),
+            key=lambda k: -min(k % inner, inner - k % inner) - min(k // inner, size // inner - k // inner),
+        )
 
     def device(section, sector):
         return {"sect": section, "sec": sector}
@@ -192,12 +205,13 @@
 
         lax.fori_loop(0, block // 16, step, 0)
 
-    def block_copy(phase, side, half):
+    def block_copy(phase, side, piece):
+        slot, start = piece // 2, (piece % 2) * (block // 2)
         return remote(
-            send_buf.at[phase, side, 2 * half : 2 * half + 2],
-            recv_buf.at[phase, 2 * half : 2 * half + 2, side * block : (side + 1) * block],
-            b_send.at[phase, side, half],
-            b_recv.at[phase, side, half],
+            send_buf.at[phase, side, slot, start : start + block // 2],
+            recv_buf.at[phase, slot, side * block + start : side * block + start + block // 2],
+            b_send.at[phase, side, piece],
+            b_recv.at[phase, side, piece],
             device(sect, (down, up)[side]),
         )
 
@@ -207,14 +221,10 @@
 
         mix(v, [(spin, w) for spin in ((0, 3), (1, 2))[half] for w in (3, 4)], store)
 
-    def send(phase, half):
-        for side in range(2):
-            block_copy(phase, side, half).start()
-
-    def sent(phase):
-        for half in range(2):
+    def send(phase, first, last):
+        for piece in range(first, last):
             for side in range(2):
-                block_copy(phase, side, half).wait_send()
+                block_copy(phase, side, piece).start()
 
     def local(phase, v):
         def store(spin, channel, rows, i, value):
@@ -229,16 +239,16 @@
             )
 
     def consume(phase):
-        for half in range(2):
-            for side in range(2):
-                block_copy(phase, side, half).wait_recv()
-            for slot in (2 * half, 2 * half + 1):
-                spin = SPIN_OF[slot]
-                hs[phase, spin] += jnp.dot(
-                    left_buf[:, 3 * block :],
-                    recv_buf[phase, slot],
-                    preferred_element_type=F32,
-                )
+        for slot in range(4):
+            for piece in (2 * slot, 2 * slot + 1):
+                for side in range(2):
+                    block_copy(phase, side, piece).wait_recv()
+            spin = SPIN_OF[slot]
+            hs[phase, spin] += jnp.dot(
+                left_buf[:, 3 * block :],
+                recv_buf[phase, slot],
+                preferred_element_type=F32,
+            )
 
     def over_rows(function, init):
         total = init
@@ -280,7 +290,7 @@
         copy_to, _ = sum_copies(phase)
         size, _, digit = stages[stage]
         sums[stage][phase, digit] = total
-        for k in range(1, size):
+        for k in far_first(size):
             copy_to(stage, k).start()
 
     def take_sums(phase, stage):
@@ -295,7 +305,8 @@
 
     def begin_sum(phase, values):
         rows = [folded_rows(value) for value in values]
-        rows.append(jnp.zeros((8 - len(rows), 128), F32))
+        if len(rows) < 8:
+            rows.append(jnp.zeros((8 - len(rows), 128), F32))
         send_sums(phase, 0, jnp.concatenate(rows, axis=0))
 
     def pass_sum(phase):
@@ -304,7 +315,7 @@
 
     def end_sum(phase):
         total = jnp.sum(take_sums(phase, len(sizes) - 1), axis=1, keepdims=True)
-        return [total[k : k + 1, :] for k in range(3)]
+        return [total[k : k + 1, :] for k in range(6)]
 
     def start_block(v, spin, rows):
         value = us[v, spin, rows, :].astype(F32)
@@ -419,7 +430,7 @@
     start_sq = [start_sum(v) for v in range(2)]
     pl.semaphore_wait(barrier, len(greeted))
     begin_sum(0, start_sq)
-    for copy in right_copies + left_copies:
+    for copy in right_copies[:4] + left_copies:
         copy.start()
     for (w2, spin, channel, spin_in), index in COEF_AT.items():
         there = sec + (CHARGE[spin_in] - 1)
@@ -428,6 +439,8 @@
         coef[index] = mpo_ref[channel, spin][spin_in, w2] * jnp.where(keep, 1.0, 0.0).astype(F32)
 
     pass_sum(0)
+    for copy in right_copies[4:]:
+        copy.start()
     right_copy(1, 0).wait_recv()
     right_copy(1, 1).wait_recv()
     start_sq = end_sum(0)
@@ -439,16 +452,17 @@
     multiply(0, 0, (0, 1), (3, 5))
     multiply(0, 0, (3, 4), (3, 5))
     produce(0, 0, 0)
+    send(0, 0, 4)
+    make_first(1, start_sq[1])
     right_copy(0, 1).wait_recv()
     right_copy(2, 1).wait_recv()
-    send(0, 0)
     multiply(0, 0, (0, 1), (0, 3))
     multiply(0, 0, (3, 4), (0, 3))
     produce(0, 0, 1)
-    send(0, 1)
-    make_first(1, start_sq[1])
+    send(0, 4, 8)
     multiply_all(1, 1)
     produce(1, 1, 0)
+    send(1, 0, 2)
     produce(1, 1, 1)
     for copy in left_copies:
         copy.wait_recv()
@@ -462,43 +476,48 @@
         left_buf[:, 4 * block :] = jnp.zeros((block, block), BF16)
 
     local(0, 0)
-    sent(0)
-    send(1, 0)
-    send(1, 1)
     consume(0)
     begin_sum(1, first_sums(0))
+    send(1, 2, 5)
     local(1, 1)
     pass_sum(1)
-    make_second(0, *end_sum(1))
+    send(1, 5, 8)
+    make_second(0, *end_sum(1)[:3])
 
     multiply_all(2, 0)
     produce(2, 0, 0)
-    sent(1)
-    send(2, 0)
-    produce(2, 0, 1)
-    send(2, 1)
+    send(2, 0, 2)
     consume(1)
     begin_sum(2, first_sums(1))
+    send(2, 2, 4)
+    produce(2, 0, 1)
+    send(2, 4, 5)
     local(2, 0)
     pass_sum(2)
-    make_second(1, *end_sum(2))
+    send(2, 5, 8)
+    make_second(1, *end_sum(2)[:3])
     multiply_all(3, 1)
     produce(3, 1, 0)
-    sent(2)
-    send(3, 0)
+    send(3, 0, 4)
     produce(3, 1, 1)
-    send(3, 1)
+    send(3, 4, 8)
+    local(3, 1)
     consume(2)
-    begin_sum(3, (kept[0, 2], *second_sums(0)))
-    local(3, 1)
+    first = (kept[0, 2], *second_sums(0))
+    consume(3)
+    begin_sum(3, (*first, kept[1, 2], *second_sums(1)))
     pass_sum(3)
-    finish(0, *end_sum(3))
-    consume(3)
-    begin_sum(4, (kept[1, 2], *second_sums(1)))
-    pass_sum(4)
-    finish(1, *end_sum(4))
-
-    sent(3)
+    final = end_sum(3)
+    finish(0, *final[:3])
+    finish(1, *final[3:])
+
+    def blocks_sent(phase, carry):
+        for piece in range(8):
+            for side in range(2):
+                block_copy(phase, side, piece).wait_send()
+        return carry
+
+    lax.fori_loop(0, 4, blocks_sent, 0)
     for copy in right_copies + left_copies:
         copy.wait_send()
 
@@ -509,7 +528,7 @@
                 copy_to(stage, k).wait_send()
         return carry
 
-    lax.fori_loop(0, 5, sums_sent, 0)
+    lax.fori_loop(0, 4, sums_sent, 0)
     for v in range(2):
         for spin in range(4):
             for copy in out_copies(v, spin):
@@ -553,12 +572,12 @@
             dma((3, 2)),
             dma((5,)),
             dma((5,)),
-            dma((4, 2, 2)),
-            dma((4, 2, 2)),
-            dma((5, len(sizes), max(sizes))),
-            dma((5, len(sizes), max(sizes))),
+            dma((4, 2, 8)),
+            dma((4, 2, 8)),
+            dma((4, len(sizes), max(sizes))),
+            dma((4, len(sizes), max(sizes))),
             dma((2, 2, 4)),
-            *[pltpu.VMEM((5, size, 8, 128), F32) for size in sizes],
+            *[pltpu.VMEM((4, size, 8, 128), F32) for size in sizes],
         ],
         compiler_params=pltpu.CompilerParams(
             collective_id=0, has_side_effects=True, vmem_limit_bytes=56 * 1024 * 1024

time: 126 us -> 112 us (0.89)
  Pallas kernels: 120 us -> 106 us
    pallas_call x1, Pallas kernels: 120 us -> 106 us  [body(): pl.pallas_call(lambda *refs: kernel(sizes, *refs), name='davidson', out_s...]
where the time goes in v3:
time: 112 us; the launch traced here: 111 us
  Pallas kernels  106 us (95%)
  local copies, waits for them, and re-layouts  5.03 us (4%)
    pallas_call x1, Pallas kernels, body(): pl.pallas_call(lambda *refs: kernel(sizes, *refs), name='davidson', out_s...  106 us
    unnamed x7, local copies, waits for them, and re-layouts  5.03 us

profile of v3, /device:TPU:2, one launch (start us, length us, event | category | flops | bytes accessed | tf_op | source)
XLA Modules:
  0.0 111.3 jit_solution(11867677154722190731)
XLA Ops:
  0.6 105.7 %davidson.1 = (f32[1,2,1,4,256,256]{5,4,3,2,1,0:T(8,128)}, f32[1,2,1,4,256,256]{5,4,3,2,1,0:T(8,128)}, f32[1,2]{1,0:T(1,128)}) custom-call(f32[5,4,4,5]{3,2,1,0:T(4,128)} %bitcast.1, bf16[1,2,1,4,256,256]{5,4,3,2,1,0:T(8,128)(2,1)} %refs_1_.1, bf16[1,1,5,256,256]{4,3,2,1,0:T(8,128)(2,1)} %refs_2_.1, bf16[1,1,5,256,256]{4,3,2,1,0:T(8,128)(2,1)} %refs_3_.1), custom_call_target="tpu_custom_call" | custom-call | tf_op jit(solution)/shard_map/davidson/pallas_call | solution.py:547
  106.3 0.0 copy-start
  106.3 3.2 %copy.10 = f32[1,2,1,4,256,256]{5,4,3,2,1,0:T(8,128)} copy(f32[1,2,1,4,256,256]{5,4,3,2,1,0:T(8,128)} %get-tuple-element.6) | data formatting | bytes 4194304
  109.5 0.0 copy-done
  109.5 0.0 copy-start.1
  109.5 1.3 %copy.11 = f32[1,2,1,4,256,256]{5,4,3,2,1,0:T(8,128)} copy(f32[1,2,1,4,256,256]{5,4,3,2,1,0:T(8,128)S(1)} %copy-done) | data formatting | bytes 4194304
  110.8 0.0 copy-done.1
  110.8 0.5 copy.12
Async XLA Ops:
  106.3 3.2 %copy-start = (f32[1,2,1,4,256,256]{5,4,3,2,1,0:T(8,128)S(1)}, f32[1,2,1,4,256,256]{5,4,3,2,1,0:T(8,128)}, u32[]{:S(2)}) copy-start(f32[1,2,1,4,256,256]{5,4,3,2,1,0:T(8,128)} %get-tuple-element.7) | copy-start | bytes 6291460
  109.5 1.3 %copy-start.1 = (f32[1,2]{1,0:T(1,128)S(1)}, f32[1,2]{1,0:T(1,128)}, u32[]{:S(2)}) copy-start(f32[1,2]{1,0:T(1,128)} %get-tuple-element.8) | copy-start | bytes 28

commit v4 on v3

--- a/solution.py
+++ b/solution.py
@@ -57,19 +57,16 @@
     start_ref,
     left_ref,
     right_ref,
-    vector_ref,
-    residual_ref,
-    energy_ref,
+    xs,
+    hs,
+    scalar_ref,
     us,
-    xs,
     part,
     right_buf,
     left_buf,
     blended,
     send_buf,
     recv_buf,
-    hs,
-    out_buf,
     kept,
     coef,
     in_sem,
@@ -81,7 +78,6 @@
     b_recv,
     ar_send,
     ar_recv,
-    out_sem,
     *sums,
 ):
     count = 1
@@ -379,14 +375,6 @@
 
         return over_rows(step, (zero, zero))
 
-    def out_copies(v, spin):
-        return [
-            pltpu.make_async_copy(
-                out_buf.at[which, v, spin], target.at[0, v, 0, spin], out_sem.at[which, v, spin]
-            )
-            for which, target in enumerate((vector_ref, residual_ref))
-        ]
-
     def finish(v, residual_sq, coupling_raw, diagonal_raw):
         rayleigh = kept[v, 0, 0:1, 0:1]
         scale = kept[v, 1, 0:1, 0:1] / jnp.sqrt(residual_sq + EPSILON)
@@ -405,25 +393,8 @@
         sine = jnp.where(flat, 0.0, sign * jnp.where(ahead, smaller, larger))
         from_second = -sine * scale
 
-        for spin in range(4):
-
-            def step(i, carry, spin=spin):
-                rows = pl.ds(pl.multiple_of(i * step_rows, step_rows), step_rows)
-                x = xs[v, spin, rows, :].astype(F32)
-                second = xs[v + 2, spin, rows, :].astype(F32)
-                ritz = cosine * x + from_second * second
-                out_buf[0, v, spin, rows, :] = ritz
-                out_buf[1, v, spin, rows, :] = (
-                    cosine * hs[v, spin, rows, :]
-                    + from_second * hs[v + 2, spin, rows, :]
-                    - energy * ritz
-                )
-                return carry
-
-            lax.fori_loop(0, block // step_rows, step, 0)
-            for copy in out_copies(v, spin):
-                copy.start()
-        energy_ref[0, v] = energy[0, 0]
+        for row, value in enumerate((cosine, from_second, energy)):
+            scalar_ref[v, row : row + 1, :] = jnp.broadcast_to(value, (1, 128))
 
     for load in loads:
         load.wait()
@@ -529,9 +500,42 @@
         return carry
 
     lax.fori_loop(0, 4, sums_sent, 0)
+
+
+def combine(scalar_ref, xs, hs, vector_ref, residual_ref, energy_ref, out_buf, out_sem):
+    block = xs.shape[-1]
+
+    def copies(v, spin):
+        return [
+            pltpu.make_async_copy(
+                out_buf.at[which, v, spin], target.at[0, v, 0, spin], out_sem.at[which, v, spin]
+            )
+            for which, target in enumerate((vector_ref, residual_ref))
+        ]
+
+    for v in range(2):
+        cosine, from_second, energy = [scalar_ref[v, k : k + 1, 0:1] for k in range(3)]
+        for spin in range(4):
+
+            def step(i, carry, v=v, spin=spin):
+                rows = pl.ds(pl.multiple_of(i * 32, 32), 32)
+                ritz = cosine * xs[v, spin, rows, :].astype(F32)
+                ritz = ritz + from_second * xs[v + 2, spin, rows, :].astype(F32)
+                out_buf[0, v, spin, rows, :] = ritz
+                out_buf[1, v, spin, rows, :] = (
+                    cosine * hs[v, spin, rows, :]
+                    + from_second * hs[v + 2, spin, rows, :]
+                    - energy * ritz
+                )
+                return carry
+
+            lax.fori_loop(0, block // 32, step, 0)
+            for copy in copies(v, spin):
+                copy.start()
+        energy_ref[0, v] = energy[0, 0]
     for v in range(2):
         for spin in range(4):
-            for copy in out_copies(v, spin):
+            for copy in copies(v, spin):
                 copy.wait()
 
 
@@ -542,29 +546,25 @@
     wide = (1, 2, 1, 4, block, block)
     any_spec = pl.BlockSpec(memory_space=pl.ANY)
     vmem_spec = pl.BlockSpec(memory_space=pltpu.VMEM)
-    smem_spec = pl.BlockSpec(memory_space=pltpu.SMEM)
     dma = pltpu.SemaphoreType.DMA
-    return pl.pallas_call(
+    vectors, images, scalars = pl.pallas_call(
         lambda *refs: kernel(sizes, *refs),
         name="davidson",
         out_shape=(
-            jax.ShapeDtypeStruct(wide, F32),
-            jax.ShapeDtypeStruct(wide, F32),
-            jax.ShapeDtypeStruct((1, 2), F32),
+            pltpu.VMEM((4, 4, block, block), BF16),
+            pltpu.VMEM((4, 4, block, block), F32),
+            pltpu.VMEM((2, 8, 128), F32),
         ),
         in_specs=[vmem_spec, any_spec, any_spec, any_spec],
-        out_specs=(any_spec, any_spec, smem_spec),
+        out_specs=(vmem_spec, vmem_spec, vmem_spec),
         scratch_shapes=[
             pltpu.VMEM((2, 4, block, block), BF16),
-            pltpu.VMEM((4, 4, block, block), BF16),
             pltpu.VMEM((2, 4, 5, block, block), F32),
             pltpu.VMEM((3, 5, block, block), BF16),
             pltpu.VMEM((block, 5 * block), BF16),
             pltpu.VMEM((4, 3 * block, block), BF16),
             pltpu.VMEM((4, 2, 4, block, block), BF16),
             pltpu.VMEM((4, 4, 2 * block, block), BF16),
-            pltpu.VMEM((4, 4, block, block), F32),
-            pltpu.VMEM((2, 2, 4, block, block), F32),
             pltpu.VMEM((2, 3, 8, 128), F32),
             pltpu.SMEM((len(COEFS),), F32),
             dma((2,)),
@@ -576,13 +576,26 @@
             dma((4, 2, 8)),
             dma((4, len(sizes), max(sizes))),
             dma((4, len(sizes), max(sizes))),
-            dma((2, 2, 4)),
             *[pltpu.VMEM((4, size, 8, 128), F32) for size in sizes],
         ],
         compiler_params=pltpu.CompilerParams(
-            collective_id=0, has_side_effects=True, vmem_limit_bytes=56 * 1024 * 1024
+            collective_id=0, has_side_effects=True, vmem_limit_bytes=48 * 1024 * 1024
         ),
     )(jnp.transpose(pair_mpo, (0, 2, 3, 1)), start_vectors, left_env, right_env)
+
+    return pl.pallas_call(
+        combine,
+        name="combine",
+        out_shape=(
+            jax.ShapeDtypeStruct(wide, F32),
+            jax.ShapeDtypeStruct(wide, F32),
+            jax.ShapeDtypeStruct((1, 2), F32),
+        ),
+        in_specs=[vmem_spec, vmem_spec, vmem_spec],
+        out_specs=(any_spec, any_spec, pl.BlockSpec(memory_space=pltpu.SMEM)),
+        scratch_shapes=[pltpu.VMEM((2, 2, 4, block, block), F32), dma((2, 2, 4))],
+        compiler_params=pltpu.CompilerParams(vmem_limit_bytes=16 * 1024 * 1024),
+    )(scalars, vectors, images)
 
 
 def solution(mesh):

time: 112 us -> 107 us (0.955)
  local copies, waits for them, and re-layouts: 5.03 us -> 0 us
    unnamed x7 -> x0, local copies, waits for them, and re-layouts: 5.03 us -> none
    pallas_call x0 -> x1, Pallas kernels: none -> 3.04 us  [body(): pl.pallas_call(combine, name='combine', out_shape=(jax.ShapeDtypeStruct(w...]
    pallas_call x1, Pallas kernels: 106 us -> 103 us  [body(): pl.pallas_call(lambda *refs: kernel(sizes, *refs), name='davidson', out_s...]
where the time goes in v4:
time: 107 us
  Pallas kernels  106 us (99%)
    pallas_call x1, Pallas kernels, body(): pl.pallas_call(lambda *refs: kernel(sizes, *refs), name='davidson', out_s...  103 us
    pallas_call x1, Pallas kernels, body(): pl.pallas_call(combine, name='combine', out_shape=(jax.ShapeDtypeStruct(w...  3.04 us

profile of v4, /device:TPU:2, one launch (start us, length us, event | category | flops | bytes accessed | tf_op | source)
XLA Modules:
  0.0 106.7 jit_solution(16807139146591018793)
XLA Ops:
  0.6 103.0 %davidson.1 = (bf16[4,4,256,256]{3,2,1,0:T(8,128)(2,1)S(1)}, f32[4,4,256,256]{3,2,1,0:T(8,128)S(1)}, f32[2,8,128]{2,1,0:T(8,128)S(1)}) custom-call(f32[5,4,4,5]{3,2,1,0:T(4,128)} %bitcast.1, bf16[1,2,1,4,256,256]{5,4,3,2,1,0:T(8,128)(2,1)} %refs_1_.1, bf16[1,1,5,256,256]{4,3,2,1,0:T(8,128)(2,1)} %refs_2_.1, bf16[1,1,5,256,256]{4,3,2,1,0:T(8,128)(2,1)} %refs_3_.1), custom_call_target="tpu_custom_call" | custom-call | tf_op jit(solution)/shard_map/davidson/pallas_call | solution.py:550
  103.7 3.0 %combine.1 = (f32[1,2,1,4,256,256]{5,4,3,2,1,0:T(8,128)}, f32[1,2,1,4,256,256]{5,4,3,2,1,0:T(8,128)}, f32[1,2]{1,0:T(1,128)}) custom-call(f32[2,8,128]{2,1,0:T(8,128)S(1)} %get-tuple-element.6.scalar_ref, bf16[4,4,256,256]{3,2,1,0:T(8,128)(2,1)S(1)} %get-tuple-element.7.xs, f32[4,4,256,256]{3,2,1,0:T(8,128)S(1)} %get-tuple-element.8.hs), custom_call_target="tpu_custom_call" | custom-call | tf_op jit(solution)/shard_map/combine/pallas_call | solution.py:586

commit v5 on v4

--- a/solution.py
+++ b/solution.py
@@ -183,6 +183,16 @@
         multiply(phase, v, (0, 1), (0, 5))
         multiply(phase, v, (3, 4), (0, 5))
 
+    def multiply_early(phase, v):
+        multiply(phase, v, (0, 1), (3, 5))
+        multiply(phase, v, (3, 4), (3, 5))
+        multiply(phase, v, (1, 3), (0, 3))
+
+    def multiply_late(phase, v):
+        multiply(phase, v, (0, 1), (0, 3))
+        multiply(phase, v, (3, 4), (0, 3))
+        multiply(phase, v, (1, 3), (3, 5))
+
     def mix(v, targets, store):
         def step(i, carry):
             rows = pl.ds(pl.multiple_of(i * 16, 16), 16)
@@ -234,7 +244,19 @@
                 left_buf[:, : 3 * block], blended[spin], preferred_element_type=F32
             )
 
-    def consume(phase):
+    def spin_rows(spin, function, total):
+        def step(i, carry):
+            rows = pl.ds(pl.multiple_of(i * step_rows, step_rows), step_rows)
+            return function(spin, rows, carry)
+
+        return lax.fori_loop(0, block // step_rows, step, total)
+
+    def over_rows(function, total):
+        for spin in range(4):
+            total = spin_rows(spin, function, total)
+        return total
+
+    def consume(phase, function, total):
         for slot in range(4):
             for piece in (2 * slot, 2 * slot + 1):
                 for side in range(2):
@@ -245,16 +267,7 @@
                 recv_buf[phase, slot],
                 preferred_element_type=F32,
             )
-
-    def over_rows(function, init):
-        total = init
-        for spin in range(4):
-
-            def step(i, carry, spin=spin):
-                rows = pl.ds(pl.multiple_of(i * step_rows, step_rows), step_rows)
-                return function(spin, rows, carry)
-
-            total = lax.fori_loop(0, block // step_rows, step, total)
+            total = spin_rows(spin, function, total)
         return total
 
     zero = jnp.zeros((8, 128), F32)
@@ -301,17 +314,20 @@
 
     def begin_sum(phase, values):
         rows = [folded_rows(value) for value in values]
-        if len(rows) < 8:
-            rows.append(jnp.zeros((8 - len(rows), 128), F32))
-        send_sums(phase, 0, jnp.concatenate(rows, axis=0))
+        rows.append(jnp.zeros((8 - len(rows), 128), F32))
+        tile = jnp.sum(jnp.concatenate(rows, axis=0), axis=1, keepdims=True)
+        lane = lax.broadcasted_iota(jnp.int32, (8, 128), 1)
+        place = lax.broadcasted_iota(jnp.int32, (8, 128), 0)
+        spread = jnp.where(lane == place, jnp.broadcast_to(tile, (8, 128)), 0.0)
+        send_sums(phase, 0, jnp.sum(spread, axis=0, keepdims=True))
 
     def pass_sum(phase):
         for stage in range(1, len(sizes)):
             send_sums(phase, stage, take_sums(phase, stage - 1))
 
     def end_sum(phase):
-        total = jnp.sum(take_sums(phase, len(sizes) - 1), axis=1, keepdims=True)
-        return [total[k : k + 1, :] for k in range(6)]
+        total = take_sums(phase, len(sizes) - 1)
+        return [total[:, k : k + 1] for k in range(6)]
 
     def start_block(v, spin, rows):
         value = us[v, spin, rows, :].astype(F32)
@@ -348,7 +364,7 @@
                 image_sq + folded(image * image),
             )
 
-        return over_rows(step, (zero, zero, zero))
+        return consume(v, step, (zero, zero, zero))
 
     def make_second(v, squared, rayleigh, image_sq):
         estimate = image_sq - 2.0 * rayleigh * rayleigh + rayleigh * rayleigh * squared
@@ -373,7 +389,7 @@
             second = xs[v + 2, spin, rows, :].astype(F32)
             return mixed + folded(x * image), diagonal + folded(second * image)
 
-        return over_rows(step, (zero, zero))
+        return consume(v + 2, step, (zero, zero))
 
     def finish(v, residual_sq, coupling_raw, diagonal_raw):
         rayleigh = kept[v, 0, 0:1, 0:1]
@@ -447,40 +463,33 @@
         left_buf[:, 4 * block :] = jnp.zeros((block, block), BF16)
 
     local(0, 0)
-    consume(0)
     begin_sum(1, first_sums(0))
-    send(1, 2, 5)
+    send(1, 2, 8)
     local(1, 1)
     pass_sum(1)
-    send(1, 5, 8)
-    make_second(0, *end_sum(1)[:3])
-
-    multiply_all(2, 0)
+    first = end_sum(1)
+    begin_sum(2, first_sums(1))
+    make_second(0, *first[:3])
+
+    multiply_early(2, 0)
     produce(2, 0, 0)
-    send(2, 0, 2)
-    consume(1)
-    begin_sum(2, first_sums(1))
-    send(2, 2, 4)
+    send(2, 0, 4)
+    multiply_late(2, 0)
     produce(2, 0, 1)
-    send(2, 4, 5)
+    send(2, 4, 6)
+    pass_sum(2)
+    send(2, 6, 8)
     local(2, 0)
-    pass_sum(2)
-    send(2, 5, 8)
     make_second(1, *end_sum(2)[:3])
-    multiply_all(3, 1)
+    multiply_early(3, 1)
     produce(3, 1, 0)
     send(3, 0, 4)
+    multiply_late(3, 1)
     produce(3, 1, 1)
     send(3, 4, 8)
     local(3, 1)
-    consume(2)
     first = (kept[0, 2], *second_sums(0))
-    consume(3)
     begin_sum(3, (*first, kept[1, 2], *second_sums(1)))
-    pass_sum(3)
-    final = end_sum(3)
-    finish(0, *final[:3])
-    finish(1, *final[3:])
 
     def blocks_sent(phase, carry):
         for piece in range(8):
@@ -499,7 +508,13 @@
                 copy_to(stage, k).wait_send()
         return carry
 
-    lax.fori_loop(0, 4, sums_sent, 0)
+    lax.fori_loop(0, 3, sums_sent, 0)
+
+    pass_sum(3)
+    final = end_sum(3)
+    finish(0, *final[:3])
+    finish(1, *final[3:])
+    sums_sent(3, 0)
 
 
 def combine(scalar_ref, xs, hs, vector_ref, residual_ref, energy_ref, out_buf, out_sem):
@@ -576,7 +591,7 @@
             dma((4, 2, 8)),
             dma((4, len(sizes), max(sizes))),
             dma((4, len(sizes), max(sizes))),
-            *[pltpu.VMEM((4, size, 8, 128), F32) for size in sizes],
+            *[pltpu.VMEM((4, size, 1, 128), F32) for size in sizes],
         ],
         compiler_params=pltpu.CompilerParams(
             collective_id=0, has_side_effects=True, vmem_limit_bytes=48 * 1024 * 1024

time: 107 us -> 105 us (0.981)
  Pallas kernels: 106 us -> 104 us
    pallas_call x1, Pallas kernels: 103 us -> 101 us  [body(): pl.pallas_call(lambda *refs: kernel(sizes, *refs), name='davidson', out_s...]
where the time goes in v5:
time: 105 us
  Pallas kernels  104 us (99%)
    pallas_call x1, Pallas kernels, body(): pl.pallas_call(lambda *refs: kernel(sizes, *refs), name='davidson', out_s...  101 us
    pallas_call x1, Pallas kernels, body(): pl.pallas_call(combine, name='combine', out_shape=(jax.ShapeDtypeStruct(w...  3.04 us

profile of v5, /device:TPU:2, one launch (start us, length us, event | category | flops | bytes accessed | tf_op | source)
XLA Modules:
  0.0 104.6 jit_solution(14586727880936126641)
XLA Ops:
  0.6 100.9 %davidson.1 = (bf16[4,4,256,256]{3,2,1,0:T(8,128)(2,1)S(1)}, f32[4,4,256,256]{3,2,1,0:T(8,128)S(1)}, f32[2,8,128]{2,1,0:T(8,128)S(1)}) custom-call(f32[5,4,4,5]{3,2,1,0:T(4,128)} %bitcast.1, bf16[1,2,1,4,256,256]{5,4,3,2,1,0:T(8,128)(2,1)} %refs_1_.1, bf16[1,1,5,256,256]{4,3,2,1,0:T(8,128)(2,1)} %refs_2_.1, bf16[1,1,5,256,256]{4,3,2,1,0:T(8,128)(2,1)} %refs_3_.1), custom_call_target="tpu_custom_call" | custom-call | tf_op jit(solution)/shard_map/davidson/pallas_call | solution.py:565
  101.6 3.0 %combine.1 = (f32[1,2,1,4,256,256]{5,4,3,2,1,0:T(8,128)}, f32[1,2,1,4,256,256]{5,4,3,2,1,0:T(8,128)}, f32[1,2]{1,0:T(1,128)}) custom-call(f32[2,8,128]{2,1,0:T(8,128)S(1)} %get-tuple-element.6.scalar_ref, bf16[4,4,256,256]{3,2,1,0:T(8,128)(2,1)S(1)} %get-tuple-element.7.xs, f32[4,4,256,256]{3,2,1,0:T(8,128)S(1)} %get-tuple-element.8.hs), custom_call_target="tpu_custom_call" | custom-call | tf_op jit(solution)/shard_map/combine/pallas_call | solution.py:601

commit v6 on v5

--- a/solution.py
+++ b/solution.py
@@ -212,10 +212,9 @@
         lax.fori_loop(0, block // 16, step, 0)
 
     def block_copy(phase, side, piece):
-        slot, start = piece // 2, (piece % 2) * (block // 2)
         return remote(
-            send_buf.at[phase, side, slot, start : start + block // 2],
-            recv_buf.at[phase, slot, side * block + start : side * block + start + block // 2],
+            send_buf.at[phase, side, piece],
+            recv_buf.at[phase, piece, side * block : (side + 1) * block],
             b_send.at[phase, side, piece],
             b_recv.at[phase, side, piece],
             device(sect, (down, up)[side]),
@@ -258,9 +257,8 @@
 
     def consume(phase, function, total):
         for slot in range(4):
-            for piece in (2 * slot, 2 * slot + 1):
-                for side in range(2):
-                    block_copy(phase, side, piece).wait_recv()
+            for side in range(2):
+                block_copy(phase, side, slot).wait_recv()
             spin = SPIN_OF[slot]
             hs[phase, spin] += jnp.dot(
                 left_buf[:, 3 * block :],
@@ -439,17 +437,17 @@
     multiply(0, 0, (0, 1), (3, 5))
     multiply(0, 0, (3, 4), (3, 5))
     produce(0, 0, 0)
-    send(0, 0, 4)
+    send(0, 0, 2)
     make_first(1, start_sq[1])
     right_copy(0, 1).wait_recv()
     right_copy(2, 1).wait_recv()
     multiply(0, 0, (0, 1), (0, 3))
     multiply(0, 0, (3, 4), (0, 3))
     produce(0, 0, 1)
-    send(0, 4, 8)
+    send(0, 2, 4)
     multiply_all(1, 1)
     produce(1, 1, 0)
-    send(1, 0, 2)
+    send(1, 0, 1)
     produce(1, 1, 1)
     for copy in left_copies:
         copy.wait_recv()
@@ -464,35 +462,35 @@
 
     local(0, 0)
     begin_sum(1, first_sums(0))
-    send(1, 2, 8)
+    send(1, 1, 3)
     local(1, 1)
     pass_sum(1)
+    send(1, 3, 4)
     first = end_sum(1)
     begin_sum(2, first_sums(1))
     make_second(0, *first[:3])
 
     multiply_early(2, 0)
     produce(2, 0, 0)
-    send(2, 0, 4)
+    send(2, 0, 2)
     multiply_late(2, 0)
     produce(2, 0, 1)
-    send(2, 4, 6)
     pass_sum(2)
-    send(2, 6, 8)
+    send(2, 2, 4)
     local(2, 0)
     make_second(1, *end_sum(2)[:3])
     multiply_early(3, 1)
     produce(3, 1, 0)
-    send(3, 0, 4)
+    send(3, 0, 2)
     multiply_late(3, 1)
     produce(3, 1, 1)
-    send(3, 4, 8)
+    send(3, 2, 4)
     local(3, 1)
     first = (kept[0, 2], *second_sums(0))
     begin_sum(3, (*first, kept[1, 2], *second_sums(1)))
 
     def blocks_sent(phase, carry):
-        for piece in range(8):
+        for piece in range(4):
             for side in range(2):
                 block_copy(phase, side, piece).wait_send()
         return carry
@@ -587,8 +585,8 @@
             dma((3, 2)),
             dma((5,)),
             dma((5,)),
-            dma((4, 2, 8)),
-            dma((4, 2, 8)),
+            dma((4, 2, 4)),
+            dma((4, 2, 4)),
             dma((4, len(sizes), max(sizes))),
             dma((4, len(sizes), max(sizes))),
             *[pltpu.VMEM((4, size, 1, 128), F32) for size in sizes],

time: 105 us -> 101 us (0.962)
  Pallas kernels: 104 us -> 99.7 us
    pallas_call x1, Pallas kernels: 101 us -> 96.7 us  [body(): pl.pallas_call(lambda *refs: kernel(sizes, *refs), name='davidson', out_s...]
where the time goes in v6:
time: 101 us; the launch traced here: 100 us
  Pallas kernels  99.7 us (99%)
    pallas_call x1, Pallas kernels, body(): pl.pallas_call(lambda *refs: kernel(sizes, *refs), name='davidson', out_s...  96.7 us
    pallas_call x1, Pallas kernels, body(): pl.pallas_call(combine, name='combine', out_shape=(jax.ShapeDtypeStruct(w...  3.04 us

profile of v6, /device:TPU:2, one launch (start us, length us, event | category | flops | bytes accessed | tf_op | source)
XLA Modules:
  0.0 100.4 jit_solution(9028380431352053153)
XLA Ops:
  0.6 96.7 %davidson.1 = (bf16[4,4,256,256]{3,2,1,0:T(8,128)(2,1)S(1)}, f32[4,4,256,256]{3,2,1,0:T(8,128)S(1)}, f32[2,8,128]{2,1,0:T(8,128)S(1)}) custom-call(f32[5,4,4,5]{3,2,1,0:T(4,128)} %bitcast.1, bf16[1,2,1,4,256,256]{5,4,3,2,1,0:T(8,128)(2,1)} %refs_1_.1, bf16[1,1,5,256,256]{4,3,2,1,0:T(8,128)(2,1)} %refs_2_.1, bf16[1,1,5,256,256]{4,3,2,1,0:T(8,128)(2,1)} %refs_3_.1), custom_call_target="tpu_custom_call" | custom-call | tf_op jit(solution)/shard_map/davidson/pallas_call | solution.py:563
  97.3 3.0 %combine.1 = (f32[1,2,1,4,256,256]{5,4,3,2,1,0:T(8,128)}, f32[1,2,1,4,256,256]{5,4,3,2,1,0:T(8,128)}, f32[1,2]{1,0:T(1,128)}) custom-call(f32[2,8,128]{2,1,0:T(8,128)S(1)} %get-tuple-element.6.scalar_ref, bf16[4,4,256,256]{3,2,1,0:T(8,128)(2,1)S(1)} %get-tuple-element.7.xs, f32[4,4,256,256]{3,2,1,0:T(8,128)S(1)} %get-tuple-element.8.hs), custom_call_target="tpu_custom_call" | custom-call | tf_op jit(solution)/shard_map/combine/pallas_call | solution.py:599
